TPU v7x, 512 devices: a whole 4x8x8 slice. The times are simulated.
512 devices in a mesh: chan: 64 (over z, x, core), win: 8 (over y).
Axes of the slice: x: 4, y: 8, z: 8, core: 2. Of those that a mesh axis runs over, the one named last changes fastest.
Arguments:
- records: bfloat16 [32, 32768, 512], P('win', 'chan'), may hold values from -6 to 6
- block_pairs: int32 [2048, 2], P('chan'), may hold values from 0 to 255, as said below
- lag_low: int32 [2048], P('chan'), may hold values from 0 to 31
- lag_high: int32 [2048], P('chan'), may hold values from 97 to 128
- slot_count: int32 [64], P('chan'), may hold values from 1 to 32, as said below
Outputs:
- stacks: float32 [2048, 128, 128], P(('chan', 'win'))
Inputs may be any that keep to these rules, and one draw needn't show every extreme that they name: `block_pairs`: slot p belongs to owner p // 32; for owner o both blocks of each slot lie within o * 4 - 16 to o * 4 + 19, and the two blocks differ by at most 16. Slots of owner o at or after slot_count[o] are unused; some owner uses all 32.
All inputs are finite; a program needn't handle non-finite values.
Results may differ from a plain program's by a relative error of at most 0.0015.
Values may be sent and summed in bfloat16 or wider, within the bound.
A program may use at most 128 MiB of HBM per device.

v0:
```python
import math

import jax
import jax.numpy as jnp
from jax import lax
from jax.sharding import PartitionSpec as P

BLOCK = 128
F = 128
LAGS = 128
REACH = 16
B_DEV = 4


def shifted(block, axis, distance):
    devices = range(lax.axis_size(axis))
    route = [(i - distance, i) for i in devices if i - distance in devices]
    return lax.ppermute(block, axis, route)


def forward_table(length, bins):
    first = length // 32
    times = jnp.arange(length, dtype=jnp.int32)[:, None]
    freqs = (first + jnp.arange(bins, dtype=jnp.int32))[None, :]
    phase = 2.0 * math.pi / length * (times * freqs % length).astype(jnp.float32)
    return jnp.concatenate([jnp.cos(phase), -jnp.sin(phase)], axis=1).astype(jnp.bfloat16)


def inverse_table(length, bins, lag_total):
    first = length // 32
    freqs = (first + jnp.arange(bins, dtype=jnp.int32))[:, None]
    shifts = (jnp.arange(lag_total, dtype=jnp.int32) - lag_total // 2)[None, :]
    phase = 2.0 * math.pi / length * (freqs * shifts % length).astype(jnp.float32)
    return jnp.concatenate([jnp.cos(phase), -jnp.sin(phase)], axis=0)


def whiten(spectra, bins):
    real_part = spectra[..., :bins]
    imag_part = spectra[..., bins:]
    power = real_part * real_part + imag_part * imag_part
    level = jnp.mean(power, axis=-1, keepdims=True)
    factor = lax.rsqrt(power + 0.1 * level + 1e-06)
    return jnp.concatenate([real_part * factor, imag_part * factor], axis=-1).astype(jnp.bfloat16)


def pair_products(first, second, bins):
    first_re, first_im = (first[..., :bins], first[..., bins:])
    second_re, second_im = (second[..., :bins], second[..., bins:])
    form = "spbf,spbf->pbf"
    real_sum = jnp.einsum(
        form, first_re, second_re, preferred_element_type=jnp.float32
    ) + jnp.einsum(form, first_im, second_im, preferred_element_type=jnp.float32)
    imag_sum = jnp.einsum(
        form, first_re, second_im, preferred_element_type=jnp.float32
    ) - jnp.einsum(form, first_im, second_re, preferred_element_type=jnp.float32)
    return jnp.concatenate([real_sum, imag_sum], axis=-1)


def per_device(records, block_pairs, lag_low, lag_high, slot_count):
    seg_count, chan_count, length = records.shape
    forward = forward_table(length, F)
    spectra = jnp.dot(
        records.reshape(seg_count * chan_count, length), forward, preferred_element_type=jnp.float32
    )
    whitened = whiten(spectra.reshape(seg_count, chan_count, 2 * F), F)
    depth = REACH // B_DEV
    pieces = []
    for offset in range(-depth, depth + 1):
        if offset == 0:
            pieces.append(whitened)
        else:
            pieces.append(shifted(whitened, "chan", -offset))
    neighbourhood = jnp.concatenate(pieces, axis=1)
    blocks = neighbourhood.reshape(seg_count, neighbourhood.shape[1] // BLOCK, BLOCK, 2 * F)
    base = (lax.axis_index("chan") - depth) * B_DEV
    slot_total = block_pairs.shape[0]
    groups = 4
    local_pairs = (block_pairs - base).reshape(groups, slot_total // groups, 2)

    def one_group(pair_rows):
        first = jnp.take(blocks, pair_rows[:, 0], axis=1)
        second = jnp.take(blocks, pair_rows[:, 1], axis=1)
        return pair_products(first, second, F)

    spectrum = lax.map(one_group, local_pairs).reshape(slot_total, BLOCK, 2 * F)
    inverse = inverse_table(length, F, LAGS)
    factor = 1.0 / math.sqrt(F * seg_count * lax.axis_size("win"))
    lag_index = jnp.arange(LAGS, dtype=jnp.int32)
    summed = lax.psum_scatter(spectrum, "win", scatter_dimension=0, tiled=True)
    share = summed.shape[0]
    start = lax.axis_index("win") * share
    slot_index = start + jnp.arange(share, dtype=jnp.int32)
    low = lax.dynamic_slice_in_dim(lag_low, start, share)
    high = lax.dynamic_slice_in_dim(lag_high, start, share)
    stack = (
        jnp.einsum(
            "pbf,fl->pbl",
            summed,
            inverse,
            precision=lax.Precision.HIGHEST,
            preferred_element_type=jnp.float32,
        )
        * factor
    )
    used = slot_index < slot_count[0]
    keep = (
        (lag_index[None, :] >= low[:, None]) & (lag_index[None, :] < high[:, None]) & used[:, None]
    )
    return jnp.where(keep[:, None, :], stack, jnp.zeros_like(stack))


def solution(mesh):
    in_specs = (P("win", "chan", None), P("chan", None), P("chan"), P("chan"), P("chan"))
    out_specs = P(("chan", "win"), None, None)
    return jax.shard_map(
        per_device, mesh=mesh, in_specs=in_specs, out_specs=out_specs, check_vma=False
    )
```

profile of v0, /device:TPU:1, one launch (start us, length us, event | category | flops | bytes accessed | tf_op | source)
XLA Modules:
  0.0 300.7 jit_solution(6856167808986573251)
XLA Ops:
  10.3 3.6 %reshape.90 = f32[4,512,256]{1,0,2:T(4,128)} reshape(f32[2048,256]{0,1:T(8,128)} %convolution_bitcast_fusion) | data formatting | bytes 4194304 | tf_op jit(solution)/shard_map/reshape | solution.py:65
  18.3 6.5 %collective-permute-start = (bf16[4,512,256]{1,0,2:T(4,128)(2,1)}, bf16[4,512,256]{1,0,2:T(4,128)(2,1)}, u32[]{:S(2)}, u32[]{:S(2)}) collective-permute-start(bf16[4,512,256]{1,0,2:T(4,128)(2,1)} %pad_maximum_fusion), channel_id=1, source_target_pairs={{0,32},{8,40},{16,48},{24,56},{32,64},{40,72},{48,80},{56,88},{64,... | collective-permute-start | bytes 3145736 | tf_op jit(solution)/shard_map/ppermute | solution.py:18
  24.8 4.8 %collective-permute-start.1 = (bf16[4,512,256]{1,0,2:T(4,128)(2,1)}, bf16[4,512,256]{1,0,2:T(4,128)(2,1)}, u32[]{:S(2)}, u32[]{:S(2)}) collective-permute-start(bf16[4,512,256]{1,0,2:T(4,128)(2,1)} %pad_maximum_fusion), channel_id=1, source_target_pairs={{0,24},{8,32},{16,40},{24,48},{32,56},{40,64},{48,72},{56,80},{64,... | collective-permute-start | bytes 3145736 | tf_op jit(solution)/shard_map/ppermute | solution.py:18
  29.6 3.1 %collective-permute-start.2 = (bf16[4,512,256]{1,0,2:T(4,128)(2,1)}, bf16[4,512,256]{1,0,2:T(4,128)(2,1)}, u32[]{:S(2)}, u32[]{:S(2)}) collective-permute-start(bf16[4,512,256]{1,0,2:T(4,128)(2,1)} %pad_maximum_fusion), channel_id=1, source_target_pairs={{0,16},{8,24},{16,32},{24,40},{32,48},{40,56},{48,64},{56,72},{64,... | collective-permute-start | bytes 3145736 | tf_op jit(solution)/shard_map/ppermute | solution.py:18
  34.6 3.4 %collective-permute-start.4 = (bf16[4,512,256]{1,0,2:T(4,128)(2,1)}, bf16[4,512,256]{1,0,2:T(4,128)(2,1)}, u32[]{:S(2)}, u32[]{:S(2)}) collective-permute-start(bf16[4,512,256]{1,0,2:T(4,128)(2,1)} %pad_maximum_fusion), channel_id=1, source_target_pairs={{8,0},{16,8},{24,16},{32,24},{40,32},{48,40},{56,48},{64,56},{72,6... | collective-permute-start | bytes 3145736 | tf_op jit(solution)/shard_map/ppermute | solution.py:18
  38.0 6.1 %collective-permute-done = bf16[4,512,256]{1,0,2:T(4,128)(2,1)} collective-permute-done((bf16[4,512,256]{1,0,2:T(4,128)(2,1)}, bf16[4,512,256]{1,0,2:T(4,128)(2,1)}, u32[]{:S(2)}, u32[]{:S(2)}) %collective-permute-start) | collective-permute-done | bytes 1048608 | tf_op jit(solution)/shard_map/ppermute | solution.py:18
  45.5 21.2 %collective-permute-done.1 = bf16[4,512,256]{1,0,2:T(4,128)(2,1)} collective-permute-done((bf16[4,512,256]{1,0,2:T(4,128)(2,1)}, bf16[4,512,256]{1,0,2:T(4,128)(2,1)}, u32[]{:S(2)}, u32[]{:S(2)}) %collective-permute-start.1) | collective-permute-done | bytes 1048608 | tf_op jit(solution)/shard_map/ppermute | solution.py:18
  68.0 21.1 %collective-permute-done.2 = bf16[4,512,256]{1,0,2:T(4,128)(2,1)} collective-permute-done((bf16[4,512,256]{1,0,2:T(4,128)(2,1)}, bf16[4,512,256]{1,0,2:T(4,128)(2,1)}, u32[]{:S(2)}, u32[]{:S(2)}) %collective-permute-start.2) | collective-permute-done | bytes 1048608 | tf_op jit(solution)/shard_map/ppermute | solution.py:18
  93.0 2.7 constant_dynamic-update-slice_fusion.7
  95.7 2.7 constant_dynamic-update-slice_fusion.6
  98.3 5.3 %collective-permute-done.3 = bf16[4,512,256]{1,0,2:T(4,128)(2,1)} collective-permute-done((bf16[4,512,256]{1,0,2:T(4,128)(2,1)}, bf16[4,512,256]{1,0,2:T(4,128)(2,1)}, u32[]{:S(2)}, u32[]{:S(2)}) %collective-permute-start.3) | collective-permute-done | bytes 1048608 | tf_op jit(solution)/shard_map/ppermute | solution.py:18
  107.8 2.7 constant_dynamic-update-slice_fusion.3
  114.2 2.8 constant_dynamic-update-slice_fusion.1
  118.4 15.3 %copy.6 = bf16[4,4608,256]{2,1,0:T(8,128)(2,1)} copy(bf16[4,4608,256]{1,0,2:T(4,128)(2,1)} %constant_dynamic-update-slice_fusion) | data formatting | bytes 18874368 | tf_op jit(solution)/shard_map/concatenate | solution.py:73
  133.7 64.9 %while.10 = (s32[]{:T(128)}, f32[4,8,128,256]{3,2,1,0:T(8,128)}, s32[4,8,2]{1,0,2:T(4,128)S(1)}, bf16[4,36,128,256]{3,2,1,0:T(8,128)(2,1)}, s32[]{:T(128)}) while((s32[]{:T(128)}, f32[4,8,128,256]{3,2,1,0:T(8,128)}, s32[4,8,2]{1,0,2:T(4,128)S(1)}, bf16[4,36,128,256]{3,2,1,0:T(8,128)(2,1)}, s32[]{:T(128)}) %tuple.44), condition=%wide.region_2.4_spmd, body=%wide.region_1.3_spmd.sunk | while | flops 8390754 | bytes 28320736 | solution.py:85
  133.7 5.7 %gather_fusion = bf16[8,4,128,256]{3,2,1,0:T(8,128)(2,1)} fusion(bf16[4,36,128,256]{3,2,1,0:T(8,128)(2,1)} %get-tuple-element.121, s32[1024]{0:T(1024)S(1)} %pad_clamp_fusion.4), kind=kCustom, calls=%fused_computation.1.clone.clone.1 | custom fusion | bytes 4194336 | tf_op jit(solution)/shard_map/while/body/eval_jaxpr/jit(_take)/gather | solution.py:82
  139.4 5.8 %gather_fusion.1 = bf16[8,4,128,256]{3,2,1,0:T(8,128)(2,1)} fusion(bf16[4,36,128,256]{3,2,1,0:T(8,128)(2,1)} %get-tuple-element.121, s32[1024]{0:T(1024)S(1)} %pad_clamp_fusion.5), kind=kCustom, calls=%fused_computation.clone.clone.1 | custom fusion | bytes 4194336 | tf_op jit(solution)/shard_map/while/body/eval_jaxpr/jit(_take)/gather | solution.py:81
  149.9 5.7 %gather_fusion = bf16[8,4,128,256]{3,2,1,0:T(8,128)(2,1)} fusion(bf16[4,36,128,256]{3,2,1,0:T(8,128)(2,1)} %get-tuple-element.121, s32[1024]{0:T(1024)S(1)} %pad_clamp_fusion.4), kind=kCustom, calls=%fused_computation.1.clone.clone.1 | custom fusion | bytes 4194336 | tf_op jit(solution)/shard_map/while/body/eval_jaxpr/jit(_take)/gather | solution.py:82
  155.6 5.8 %gather_fusion.1 = bf16[8,4,128,256]{3,2,1,0:T(8,128)(2,1)} fusion(bf16[4,36,128,256]{3,2,1,0:T(8,128)(2,1)} %get-tuple-element.121, s32[1024]{0:T(1024)S(1)} %pad_clamp_fusion.5), kind=kCustom, calls=%fused_computation.clone.clone.1 | custom fusion | bytes 4194336 | tf_op jit(solution)/shard_map/while/body/eval_jaxpr/jit(_take)/gather | solution.py:81
  166.2 5.7 %gather_fusion = bf16[8,4,128,256]{3,2,1,0:T(8,128)(2,1)} fusion(bf16[4,36,128,256]{3,2,1,0:T(8,128)(2,1)} %get-tuple-element.121, s32[1024]{0:T(1024)S(1)} %pad_clamp_fusion.4), kind=kCustom, calls=%fused_computation.1.clone.clone.1 | custom fusion | bytes 4194336 | tf_op jit(solution)/shard_map/while/body/eval_jaxpr/jit(_take)/gather | solution.py:82
  171.9 5.8 %gather_fusion.1 = bf16[8,4,128,256]{3,2,1,0:T(8,128)(2,1)} fusion(bf16[4,36,128,256]{3,2,1,0:T(8,128)(2,1)} %get-tuple-element.121, s32[1024]{0:T(1024)S(1)} %pad_clamp_fusion.5), kind=kCustom, calls=%fused_computation.clone.clone.1 | custom fusion | bytes 4194336 | tf_op jit(solution)/shard_map/while/body/eval_jaxpr/jit(_take)/gather | solution.py:81
  182.4 5.7 %gather_fusion = bf16[8,4,128,256]{3,2,1,0:T(8,128)(2,1)} fusion(bf16[4,36,128,256]{3,2,1,0:T(8,128)(2,1)} %get-tuple-element.121, s32[1024]{0:T(1024)S(1)} %pad_clamp_fusion.4), kind=kCustom, calls=%fused_computation.1.clone.clone.1 | custom fusion | bytes 4194336 | tf_op jit(solution)/shard_map/while/body/eval_jaxpr/jit(_take)/gather | solution.py:82
  188.1 5.8 %gather_fusion.1 = bf16[8,4,128,256]{3,2,1,0:T(8,128)(2,1)} fusion(bf16[4,36,128,256]{3,2,1,0:T(8,128)(2,1)} %get-tuple-element.121, s32[1024]{0:T(1024)S(1)} %pad_clamp_fusion.5), kind=kCustom, calls=%fused_computation.clone.clone.1 | custom fusion | bytes 4194336 | tf_op jit(solution)/shard_map/while/body/eval_jaxpr/jit(_take)/gather | solution.py:81
  200.5 91.0 %reduce-scatter.2.cloned.1.call-done = f32[4,128,256]{2,1,0:T(8,128)} async-done(((f32[32,128,256]{2,1,0:T(8,128)}), f32[4,128,256]{2,1,0:T(8,128)}) %reduce-scatter.2.cloned.1.call-update) | async-done | bytes 524304 | tf_op jit(solution)/shard_map/reduce_scatter | solution.py:89
  (77 shorter events, 48.4 us)
Async XLA Ops:
  6.5 1.6 copy-start
  6.5 284.9 %reduce-scatter.2.cloned.1.call-start = ((), (), s32[]{:S(2)}) async-start(), calls=%async_computation.1 | async-start | bytes 4718592 | tf_op jit(solution)/shard_map/reduce_scatter | solution.py:89
  13.9 2.2 copy-start.1
  13.9 54.0 %copy-start.2 = (s32[32,2]{0,1:T(2,128)S(1)}, s32[32,2]{0,1:T(2,128)}, u32[]{:S(2)}) copy-start(s32[32,2]{0,1:T(2,128)} %param.10) | copy-start | bytes 772
  18.3 25.9 %collective-permute-start = (bf16[4,512,256]{1,0,2:T(4,128)(2,1)}, bf16[4,512,256]{1,0,2:T(4,128)(2,1)}, u32[]{:S(2)}, u32[]{:S(2)}) collective-permute-start(bf16[4,512,256]{1,0,2:T(4,128)(2,1)} %pad_maximum_fusion), channel_id=1, source_target_pairs={{0,32},{8,40},{16,48},{24,56},{32,64},{40,72},{48,80},{56,88},{64,... | collective-permute-start | bytes 3145736 | tf_op jit(solution)/shard_map/ppermute | solution.py:18
  24.8 41.8 %collective-permute-start.1 = (bf16[4,512,256]{1,0,2:T(4,128)(2,1)}, bf16[4,512,256]{1,0,2:T(4,128)(2,1)}, u32[]{:S(2)}, u32[]{:S(2)}) collective-permute-start(bf16[4,512,256]{1,0,2:T(4,128)(2,1)} %pad_maximum_fusion), channel_id=1, source_target_pairs={{0,24},{8,32},{16,40},{24,48},{32,56},{40,64},{48,72},{56,80},{64,... | collective-permute-start | bytes 3145736 | tf_op jit(solution)/shard_map/ppermute | solution.py:18
  29.6 59.5 %collective-permute-start.2 = (bf16[4,512,256]{1,0,2:T(4,128)(2,1)}, bf16[4,512,256]{1,0,2:T(4,128)(2,1)}, u32[]{:S(2)}, u32[]{:S(2)}) collective-permute-start(bf16[4,512,256]{1,0,2:T(4,128)(2,1)} %pad_maximum_fusion), channel_id=1, source_target_pairs={{0,16},{8,24},{16,32},{24,40},{32,48},{40,56},{48,64},{56,72},{64,... | collective-permute-start | bytes 3145736 | tf_op jit(solution)/shard_map/ppermute | solution.py:18
  32.7 70.9 %collective-permute-start.3 = (bf16[4,512,256]{1,0,2:T(4,128)(2,1)}, bf16[4,512,256]{1,0,2:T(4,128)(2,1)}, u32[]{:S(2)}, u32[]{:S(2)}) collective-permute-start(bf16[4,512,256]{1,0,2:T(4,128)(2,1)} %pad_maximum_fusion), channel_id=1, source_target_pairs={{0,8},{8,16},{16,24},{24,32},{32,40},{40,48},{48,56},{56,64},{64,7... | collective-permute-start | bytes 3145736 | tf_op jit(solution)/shard_map/ppermute | solution.py:18
  34.6 73.2 %collective-permute-start.4 = (bf16[4,512,256]{1,0,2:T(4,128)(2,1)}, bf16[4,512,256]{1,0,2:T(4,128)(2,1)}, u32[]{:S(2)}, u32[]{:S(2)}) collective-permute-start(bf16[4,512,256]{1,0,2:T(4,128)(2,1)} %pad_maximum_fusion), channel_id=1, source_target_pairs={{8,0},{16,8},{24,16},{32,24},{40,32},{48,40},{56,48},{64,56},{72,6... | collective-permute-start | bytes 3145736 | tf_op jit(solution)/shard_map/ppermute | solution.py:18
  44.2 67.4 %collective-permute-start.5 = (bf16[4,512,256]{1,0,2:T(4,128)(2,1)}, bf16[4,512,256]{1,0,2:T(4,128)(2,1)}, u32[]{:S(2)}, u32[]{:S(2)}) collective-permute-start(bf16[4,512,256]{1,0,2:T(4,128)(2,1)} %pad_maximum_fusion), channel_id=1, source_target_pairs={{16,0},{24,8},{32,16},{40,24},{48,32},{56,40},{64,48},{72,56},{80,... | collective-permute-start | bytes 3145736 | tf_op jit(solution)/shard_map/ppermute | solution.py:18
  66.6 47.6 %collective-permute-start.6 = (bf16[4,512,256]{1,0,2:T(4,128)(2,1)}, bf16[4,512,256]{1,0,2:T(4,128)(2,1)}, u32[]{:S(2)}, u32[]{:S(2)}) collective-permute-start(bf16[4,512,256]{1,0,2:T(4,128)(2,1)} %pad_maximum_fusion), channel_id=1, source_target_pairs={{24,0},{32,8},{40,16},{48,24},{56,32},{64,40},{72,48},{80,56},{88,... | collective-permute-start | bytes 3145736 | tf_op jit(solution)/shard_map/ppermute | solution.py:18
  89.1 27.9 %collective-permute-start.7 = (bf16[4,512,256]{1,0,2:T(4,128)(2,1)}, bf16[4,512,256]{1,0,2:T(4,128)(2,1)S(1)}, u32[]{:S(2)}, u32[]{:S(2)}) collective-permute-start(bf16[4,512,256]{1,0,2:T(4,128)(2,1)} %pad_maximum_fusion), channel_id=1, source_target_pairs={{32,0},{40,8},{48,16},{56,24},{64,32},{72,40},{80,48},{88,56},{96,... | collective-permute-start | bytes 3145736 | tf_op jit(solution)/shard_map/ppermute | solution.py:18
  198.6 0.7 copy-start.3
  198.6 0.7 copy-start.4
Sparse Core Ops, SparseCore 0:
  198.8 92.6 reduce-scatter.1
where the time goes:
time: 302 us; the launch traced here: 301 us
  waiting for transfers between devices  146 us (48%)
  local copies, waits for them, and re-layouts  86.2 us (29%)
  other arithmetic  26.3 us (9%)
  starting transfers between devices  23.5 us (8%)
  between operations  14.2 us (5%)
  matrix products  4.45 us (1%)
    reduce_scatter x1, waiting for transfers between devices, per_device(): summed = lax.psum_scatter(spectrum, 'win', scatter_dimension=0, tiled=True)  91 us
    ppermute x8, waiting for transfers between devices, shifted(): return lax.ppermute(block, axis, route)  54.8 us
    ppermute x8, starting transfers between devices, shifted(): return lax.ppermute(block, axis, route)  23.5 us
    gather x4, local copies, waits for them, and re-layouts, one_group(): first = jnp.take(blocks, pair_rows[:, 0], axis=1)  23.1 us
    gather x4, local copies, waits for them, and re-layouts, one_group(): second = jnp.take(blocks, pair_rows[:, 1], axis=1)  22.7 us
    unnamed x17, local copies, waits for them, and re-layouts  19.8 us
    concatenate x2, local copies, waits for them, and re-layouts, per_device(): neighbourhood = jnp.concatenate(pieces, axis=1)  16.7 us
    select_n x4, other arithmetic, one_group(): second = jnp.take(blocks, pair_rows[:, 1], axis=1)  10.6 us
  transfers between devices with their start and end apart: 9, of which 6 were waited for; matrix products, arithmetic and copies ran while one was open for 7% of the time, Pallas kernels for 0%

commit v1 on v0

v1 whole, which is shorter than its diff:
```python
import math

import jax
import jax.numpy as jnp
import ml_dtypes
import numpy as np
from jax import lax
from jax.experimental import pallas as pl
from jax.experimental.pallas import tpu as pltpu
from jax.sharding import PartitionSpec as P

BLOCK = 128
NT = 512
F = 128
LAGS = 128
B_DEV = 4
PO = 32
NX = 8
NY = 8
SEGS = 4
ROWS = 16
NBLK = 64
MESH = pl.DeviceIdType.MESH
DISTANCES = (0, 1, -1, 2, -2, 3, -3, 4)


def forward_table():
    times = np.arange(NT, dtype=np.int64)[:, None]
    freqs = (NT // 32 + np.arange(F, dtype=np.int64))[None, :]
    phase = 2.0 * math.pi / NT * (times * freqs % NT)
    table = np.concatenate([np.cos(phase), -np.sin(phase)], axis=1)
    return table.astype(np.float32).astype(ml_dtypes.bfloat16)


def inverse_table():
    freqs = (NT // 32 + np.arange(F, dtype=np.int64))[:, None]
    shifts = (np.arange(LAGS, dtype=np.int64) - LAGS // 2)[None, :]
    phase = 2.0 * math.pi / NT * (freqs * shifts % NT)
    table = np.concatenate([np.cos(phase), -np.sin(phase)], axis=0)
    return (table / math.sqrt(F * SEGS * NY)).astype(np.float32)


def spectra_kernel(x_ref, fwd_ref, out_ref, re_s, im_s):
    x = x_ref[...].reshape(SEGS * BLOCK, NT)
    spec = jnp.dot(x, fwd_ref[...], preferred_element_type=jnp.float32)
    re, im = spec[:, :F], spec[:, F:]
    power = re * re + im * im
    level = jnp.mean(power, axis=-1, keepdims=True)
    factor = lax.rsqrt(power + 0.1 * level + 1e-06)
    re, im = re * factor, im * factor
    for seg in range(SEGS):
        re_s[pl.ds(seg, BLOCK, stride=SEGS), :] = re[seg * BLOCK : (seg + 1) * BLOCK]
        im_s[pl.ds(seg, BLOCK, stride=SEGS), :] = im[seg * BLOCK : (seg + 1) * BLOCK]
    both = jnp.concatenate(
        [re_s[...].reshape(NX * NY, 8, F), im_s[...].reshape(NX * NY, 8, F)], axis=1
    )
    out_ref[...] = both.astype(jnp.bfloat16).reshape(NX * NY, 1, ROWS, F)


def spectra(records):
    fwd = jnp.asarray(forward_table())
    return pl.pallas_call(
        spectra_kernel,
        grid=(B_DEV,),
        out_shape=jax.ShapeDtypeStruct((NX * NY, B_DEV, ROWS, F), jnp.bfloat16),
        in_specs=[
            pl.BlockSpec((SEGS, BLOCK, NT), lambda b: (0, b, 0)),
            pl.BlockSpec((NT, 2 * F), lambda b: (0, 0)),
        ],
        out_specs=pl.BlockSpec((NX * NY, 1, ROWS, F), lambda b: (0, b, 0, 0)),
        scratch_shapes=[pltpu.VMEM((SEGS * BLOCK, F), jnp.float32)] * 2,
    )(records, fwd)


def remote(src, dst, send, recv, chan, win):
    return pltpu.make_async_remote_copy(
        src_ref=src,
        dst_ref=dst,
        send_sem=send,
        recv_sem=recv,
        device_id=(chan, win),
        device_id_type=MESH,
    )


def place():
    chan = lax.axis_index("chan")
    win = lax.axis_index("win")
    xc = lax.rem(chan, NX)
    return chan, win, xc, chan - xc


def greet(chan, win, xc, row, z_too):
    barrier = pltpu.get_barrier_semaphore()
    for step in range(1, NY):
        pl.semaphore_signal(
            barrier, inc=1, device_id=(chan, lax.rem(win + step, NY)), device_id_type=MESH
        )
    for step in range(1, NX):
        pl.semaphore_signal(
            barrier, inc=1, device_id=(row + lax.rem(xc + step, NX), win), device_id_type=MESH
        )
    count = NY + NX - 2
    if z_too:
        total = lax.axis_size("chan")
        for step in (NX, total - NX):
            pl.semaphore_signal(
                barrier, inc=1, device_id=(lax.rem(chan + step, total), win), device_id_type=MESH
            )
        count += 2
    pl.semaphore_wait(barrier, count)


def spread_kernel(
    s_ref, p_ref, d_ref, pg_ref, e_ref,
    y_send, y_recv, x_send, x_recv, own_sem, z_send, z_recv, p_send, p_recv, p_own,
):
    chan, win, xc, row = place()
    total = lax.axis_size("chan")
    up, down = lax.rem(chan + NX, total), lax.rem(chan + total - NX, total)
    greet(chan, win, xc, row, True)

    y_copies = []
    for k, dist in enumerate(DISTANCES):
        if k:
            to = lax.rem(win + dist + NY, NY)
            copy = remote(s_ref.at[to], e_ref.at[win], y_send.at[k], y_recv.at[win], chan, to)
            copy.start()
            y_copies.append(copy)

    pairs_own = pltpu.make_async_copy(p_ref, pg_ref.at[xc], p_own)
    pairs_own.start()
    for step in range(1, NX):
        other = row + lax.rem(xc + step, NX)
        remote(p_ref, pg_ref.at[xc], p_send.at[step], p_recv.at[step], other, win).start()

    own_first = 16 + xc * B_DEV
    owns = []
    z_copies = []

    def finish(src):
        many = d_ref.at[src, pl.ds(0, (NX - 1) * B_DEV)]
        remote(many, many, x_send.at[src], x_recv.at[src], chan, win).wait_recv()
        owns[-1].wait()

    def pass_on(src):
        for side, (lo, there, to) in enumerate(((16, 48, down), (32, 0, up))):
            copy = remote(
                d_ref.at[src, pl.ds(lo, 16)], d_ref.at[src, pl.ds(there, 16)],
                z_send.at[src, side], z_recv.at[src, side], to, win,
            )
            copy.start()
            z_copies.append(copy)

    previous = None
    for k, dist in enumerate(DISTANCES):
        src = lax.rem(win + dist + NY, NY)
        if k:
            remote(s_ref.at[src], e_ref.at[src], y_send.at[k], y_recv.at[src], chan, src).wait_recv()
        held = e_ref.at[src] if k else s_ref.at[src]
        for step in range(1, NX):
            to = lax.rem(xc + step, NX)
            remote(
                held.at[to], d_ref.at[src, pl.ds(own_first, B_DEV)],
                x_send.at[src], x_recv.at[src], row + to, win,
            ).start()
        own = pltpu.make_async_copy(
            held.at[xc], d_ref.at[src, pl.ds(own_first, B_DEV)], own_sem.at[k]
        )
        own.start()
        if previous is not None:
            finish(previous)
            pass_on(previous)
        owns.append(own)
        previous = src
    finish(previous)
    pass_on(previous)

    for copy in z_copies:
        copy.wait()
    for copy in y_copies:
        copy.wait_send()
    for dist in DISTANCES:
        src = lax.rem(win + dist + NY, NY)
        many = d_ref.at[src, pl.ds(0, (NX - 1) * B_DEV)]
        remote(many, many, x_send.at[src], x_recv.at[src], chan, win).wait_send()
    pairs_own.wait()
    for step in range(1, NX):
        frm = lax.rem(xc + NX - step, NX)
        copy = remote(p_ref, pg_ref.at[frm], p_send.at[step], p_recv.at[step], row + frm, win)
        copy.wait()


def spread(slices, pairs):
    dma = pltpu.SemaphoreType.DMA
    any_spec = pl.BlockSpec(memory_space=pl.ANY)
    return pl.pallas_call(
        spread_kernel,
        out_shape=[
            jax.ShapeDtypeStruct((NY, NBLK, ROWS, F), jnp.bfloat16),
            jax.ShapeDtypeStruct((NX, 8, 128), jnp.int32),
        ],
        in_specs=[any_spec, any_spec],
        out_specs=[any_spec, any_spec],
        scratch_shapes=[
            pltpu.VMEM((NY, NX, B_DEV, ROWS, F), jnp.bfloat16),
            dma((NY,)), dma((NY,)), dma((NY,)), dma((NY,)), dma((NY,)),
            dma((NY, 2)), dma((NY, 2)), dma((NX,)), dma((NX,)), dma(()),
        ],
        compiler_params=pltpu.CompilerParams(collective_id=0, has_side_effects=True),
    )(slices, pairs)


def pair_kernel(p_ref, d_ref, inv_ref, t_ref, re_s, im_s):
    def owner(o, carry):
        def slot(j, carry):
            a, b = p_ref[o * 8, j], p_ref[o * 8, PO + j]
            real = jnp.zeros((8, F), jnp.float32)
            imag = jnp.zeros((8, F), jnp.float32)
            for y in range(NY):
                first = d_ref[y, a].astype(jnp.float32)
                second = d_ref[y, b].astype(jnp.float32)
                a_re, a_im, b_re, b_im = first[:8], first[8:], second[:8], second[8:]
                real += a_re * b_re + a_im * b_im
                imag += a_re * b_im - a_im * b_re
            at = pl.ds(pl.multiple_of((o * PO + j) * 8, 8), 8)
            re_s[at, :] = real
            im_s[at, :] = imag
            return carry

        return lax.fori_loop(0, p_ref[o * 8, 2 * PO], slot, carry)

    lax.fori_loop(0, NX, owner, 0)
    count = NX * PO * 2
    cross = jnp.concatenate(
        [sum(s[pl.ds(seg, count, stride=SEGS), :] for seg in range(SEGS)) for s in (re_s, im_s)],
        axis=1,
    )
    stack = jnp.dot(
        cross, inv_ref[...], precision=lax.Precision.HIGHEST, preferred_element_type=jnp.float32
    ).reshape(NX, NY, 8, LAGS)
    for y in range(NY):
        t_ref[y] = stack[:, y]


def pair_stacks(gathered, blocks):
    inverse = jnp.asarray(inverse_table())
    rows = NX * PO * 8
    return pl.pallas_call(
        pair_kernel,
        out_shape=jax.ShapeDtypeStruct((NY, NX, 8, LAGS), jnp.float32),
        in_specs=[
            pl.BlockSpec(memory_space=pltpu.SMEM),
            pl.BlockSpec(memory_space=pltpu.VMEM),
            pl.BlockSpec(memory_space=pltpu.VMEM),
        ],
        out_specs=pl.BlockSpec(memory_space=pltpu.VMEM),
        scratch_shapes=[pltpu.VMEM((rows, F), jnp.float32)] * 2,
    )(gathered.reshape(NX * 8, 128), blocks, inverse)


def collect_kernel(t_ref, v_ref, u_ref, x_send, x_recv, x_own, y_send, y_recv, y_own):
    chan, win, xc, row = place()
    greet(chan, win, xc, row, False)
    own = pltpu.make_async_copy(t_ref.at[:, xc], u_ref.at[xc], x_own)
    own.start()
    copies = []
    for step in range(1, NX):
        to = lax.rem(xc + step, NX)
        copy = remote(
            t_ref.at[:, to], u_ref.at[xc], x_send.at[step], x_recv.at[step], row + to, win
        )
        copy.start()
        copies.append(copy)
    own.wait()
    for copy in copies:
        copy.wait()
    own = pltpu.make_async_copy(u_ref.at[:, win], v_ref.at[win], y_own)
    own.start()
    copies = []
    for k, dist in enumerate(DISTANCES):
        if k:
            to = lax.rem(win + dist + NY, NY)
            copy = remote(
                u_ref.at[:, to], v_ref.at[win], y_send.at[k], y_recv.at[k], chan, to
            )
            copy.start()
            copies.append(copy)
    own.wait()
    for copy in copies:
        copy.wait()


def collect(stacks):
    dma = pltpu.SemaphoreType.DMA
    any_spec = pl.BlockSpec(memory_space=pl.ANY)
    return pl.pallas_call(
        collect_kernel,
        out_shape=jax.ShapeDtypeStruct((NY, NX, 8, LAGS), jnp.float32),
        in_specs=[any_spec],
        out_specs=any_spec,
        scratch_shapes=[
            pltpu.VMEM((NX, NY, 8, LAGS), jnp.float32),
            dma((NX,)), dma((NX,)), dma(()), dma((NY,)), dma((NY,)), dma(()),
        ],
        compiler_params=pltpu.CompilerParams(collective_id=1, has_side_effects=True),
    )(stacks)


def mask_kernel(low_ref, high_ref, used_ref, v_ref, out_ref):
    lag = lax.broadcasted_iota(jnp.int32, (NX * NY, LAGS), 1)
    start = lax.axis_index("win") * B_DEV
    for slot in range(PO // NY):
        here = start + slot
        high = jnp.where(here < used_ref[0], high_ref[here], 0)
        keep = (lag >= low_ref[here]) & (lag < high)
        for c in range(2):
            rows = v_ref[pl.ds(slot * 2 + c, NX * NY, stride=8), :]
            out_ref[pl.ds(slot * BLOCK + c, NX * NY, stride=2), :] = jnp.where(keep, rows, 0.0)


def masked(lag_low, lag_high, slot_count, collected):
    smem = pl.BlockSpec(memory_space=pltpu.SMEM)
    vmem = pl.BlockSpec(memory_space=pltpu.VMEM)
    share = PO // NY
    return pl.pallas_call(
        mask_kernel,
        out_shape=jax.ShapeDtypeStruct((share * BLOCK, LAGS), jnp.float32),
        in_specs=[smem, smem, smem, vmem],
        out_specs=vmem,
    )(lag_low, lag_high, slot_count, collected.reshape(NX * NY * 8, LAGS)).reshape(
        share, BLOCK, LAGS
    )


def per_device(records, block_pairs, lag_low, lag_high, slot_count):
    chan = lax.axis_index("chan")
    base = chan // NX * NX * B_DEV - 16
    packed = jnp.concatenate([block_pairs[:, 0] - base, block_pairs[:, 1] - base, slot_count])
    pairs = jnp.pad(packed, (0, 8 * 128 - packed.shape[0])).reshape(8, 128)
    slices = spectra(records).reshape(NY, NX, B_DEV, ROWS, F)
    blocks, gathered = spread(slices, pairs)
    stacks = pair_stacks(gathered, blocks)
    return masked(lag_low, lag_high, slot_count, collect(stacks))


def solution(mesh):
    in_specs = (P("win", "chan", None), P("chan", None), P("chan"), P("chan"), P("chan"))
    out_specs = P(("chan", "win"), None, None)
    return jax.shard_map(
        per_device, mesh=mesh, in_specs=in_specs, out_specs=out_specs, check_vma=False
    )
```

time: 302 us -> 84 us (0.28)
  waiting for transfers between devices: 146 us -> 0 us
  local copies, waits for them, and re-layouts: 86.2 us -> 0.6 us
  Pallas kernels: 0 us -> 81.2 us
  other arithmetic: 26.3 us -> 0.84 us
  starting transfers between devices: 23.5 us -> 0 us
  between operations: 14.2 us -> 0.67 us
  matrix products: 4.45 us -> 0 us
    reduce_scatter x1 -> x0, waiting for transfers between devices: 91 us -> none  [per_device(): summed = lax.psum_scatter(spectrum, 'win', scatter_dimension=0, tiled=True)]
    pallas_call x0 -> x5, Pallas kernels: none -> 81.2 us  [the longest x1 49.7 us: spread(): pl.pallas_call(spread_kernel, out_shape=[jax.ShapeDtypeStruct((NY, NBLK,...]
    ppermute x8 -> x0, waiting for transfers between devices: 54.8 us -> none  [shifted(): return lax.ppermute(block, axis, route)]
    gather x8 -> x0, local copies, waits for them, and re-layouts: 45.8 us -> none  [the longest x4 23.1 us: one_group(): first = jnp.take(blocks, pair_rows[:, 0], axis=1)]
    ppermute x8 -> x0, starting transfers between devices: 23.5 us -> none  [shifted(): return lax.ppermute(block, axis, route)]
    unnamed x17 -> x0, local copies, waits for them, and re-layouts: 19.8 us -> none
    concatenate x2 -> x0, local copies, waits for them, and re-layouts: 16.7 us -> none  [per_device(): neighbourhood = jnp.concatenate(pieces, axis=1)]
    select_n x4 -> x0, other arithmetic: 10.6 us -> none  [one_group(): second = jnp.take(blocks, pair_rows[:, 1], axis=1)]
  transfers between devices with their start and end apart: 9 -> 0, of which waited for: 6 -> 0; matrix products, arithmetic and copies ran while one was open for 7% -> 0% of each run, Pallas kernels for 0% -> 0%
where the time goes in v1:
time: 84 us; the launch traced here: 83.3 us
  Pallas kernels  81.2 us (97%)
  other arithmetic  0.84 us (1%)
    pallas_call x1, Pallas kernels, spread(): pl.pallas_call(spread_kernel, out_shape=[jax.ShapeDtypeStruct((NY, NBLK,...  49.7 us
    pallas_call x1, Pallas kernels, collect(): pl.pallas_call(collect_kernel, out_shape=jax.ShapeDtypeStruct((NY, NX, 8,...  18.4 us
    pallas_call x1, Pallas kernels, pair_stacks(): pl.pallas_call(pair_kernel, out_shape=jax.ShapeDtypeStruct((NY, NX, 8, LA...  6.86 us
    pallas_call x1, Pallas kernels, spectra(): pl.pallas_call(spectra_kernel, grid=(B_DEV,), out_shape=jax.ShapeDtypeStr...  4.49 us
    pallas_call x1, Pallas kernels, masked(): pl.pallas_call(mask_kernel, out_shape=jax.ShapeDtypeStruct((share * BLOCK...  1.73 us

profile of v1, /device:TPU:1, one launch (start us, length us, event | category | flops | bytes accessed | tf_op | source)
XLA Modules:
  0.0 83.3 jit_solution(8038072533973131261)
XLA Ops:
  0.7 0.8 subtract_bitcast_fusion.1
  1.4 0.1 pad_add_fusion
  1.5 0.6 pad_bitcast_fusion.p_ref
  2.1 4.5 %shard_map.73 = bf16[64,4,16,128]{3,2,1,0:T(8,128)(2,1)} custom-call(bf16[4,512,512]{2,1,0:T(8,128)(2,1)} %x_ref.1, bf16[512,256]{1,0:T(8,128)(2,1)} %constant.33.clone.fwd_ref), custom_call_target="tpu_custom_call" | custom-call | tf_op jit(solution)/shard_map/pallas_call | solution.py:62
  6.6 49.7 %shard_map.74 = (bf16[8,64,16,128]{3,2,1,0:T(8,128)(2,1)}, s32[8,8,128]{2,1,0:T(8,128)}) custom-call(bf16[8,8,4,16,128]{4,3,2,1,0:T(8,128)(2,1)} %bitcast.10, s32[8,128]{1,0:T(8,128)} %pad_bitcast_fusion.p_ref), custom_call_target="tpu_custom_call" | custom-call | tf_op jit(solution)/shard_map/pallas_call | solution.py:197
  56.3 6.9 %shard_map.75.t_ref = f32[8,8,8,128]{3,2,1,0:T(8,128)} custom-call(s32[64,128]{1,0:T(8,128)} %bitcast.12, bf16[8,64,16,128]{3,2,1,0:T(8,128)(2,1)} %get-tuple-element.8.d_ref, f32[256,128]{1,0:T(8,128)} %constant.34.clone.inv_ref), custom_call_target="tpu_custom_call" | custom-call | tf_op jit(solution)/shard_map/pallas_call | solution.py:249
  63.1 18.4 %shard_map.76 = f32[8,8,8,128]{3,2,1,0:T(8,128)} custom-call(f32[8,8,8,128]{3,2,1,0:T(8,128)} %shard_map.75.t_ref), custom_call_target="tpu_custom_call" | custom-call | tf_op jit(solution)/shard_map/pallas_call | solution.py:297
  81.6 1.7 %shard_map.77 = f32[512,128]{1,0:T(8,128)} custom-call(s32[32]{0:T(128)} %low_ref.1, s32[32]{0:T(128)} %high_ref.1, s32[1]{0:T(128)S(6)} %copy.8.used_ref, f32[512,128]{1,0:T(8,128)} %bitcast.11), custom_call_target="tpu_custom_call" | custom-call | tf_op jit(solution)/shard_map/pallas_call | solution.py:326

commit v2 on v0

v2 whole, which is shorter than its diff:
```python
import math

import jax
import jax.numpy as jnp
import ml_dtypes
import numpy as np
from jax import lax
from jax.experimental import pallas as pl
from jax.experimental.pallas import tpu as pltpu
from jax.sharding import PartitionSpec as P

BLOCK = 128
NT = 512
F = 128
LAGS = 128
B_DEV = 4
PO = 32
NX = 8
NY = 8
SEGS = 4
ROWS = 16
NBLK = 64
MESH = pl.DeviceIdType.MESH
DISTANCES = (4, 3, -3, 0, 2, -2, 1, -1)
BACK = (0, 2, 1, 3, 5, 4, 7, 6)
FAR, OWN, EARLY = 3, 3, 4
OUT_ORDER = (0, 1, 2, 4, 5, 6, 7, 3)


def forward_table():
    times = np.arange(NT, dtype=np.int64)[:, None]
    freqs = (NT // 32 + np.arange(F, dtype=np.int64))[None, :]
    phase = 2.0 * math.pi / NT * (times * freqs % NT)
    table = np.concatenate([np.cos(phase), -np.sin(phase)], axis=1)
    return table.astype(np.float32).astype(ml_dtypes.bfloat16)


def inverse_table():
    freqs = (NT // 32 + np.arange(F, dtype=np.int64))[:, None]
    shifts = (np.arange(LAGS, dtype=np.int64) - LAGS // 2)[None, :]
    phase = 2.0 * math.pi / NT * (freqs * shifts % NT)
    table = np.concatenate([np.cos(phase), -np.sin(phase)], axis=0)
    return (table / math.sqrt(F * SEGS * NY)).astype(np.float32)


def remote(src, dst, send, recv, chan, win):
    return pltpu.make_async_remote_copy(
        src_ref=src,
        dst_ref=dst,
        send_sem=send,
        recv_sem=recv,
        device_id=(chan, win),
        device_id_type=MESH,
    )


def kernel(
    x_ref, fwd_ref, inv_ref, low_ref, high_ref, used_ref, pairs_ref,
    out_ref,
    x_buf, fwd_buf, inv_buf, low_s, high_s, used_s, re_s, im_s, slices, far_in, near_in,
    early, late, re_acc, im_acc, pair_buf, pair_idx, stacks, stacks_in, rows_in,
    load_sem, yf_send, yf_recv, xf_send, xf_recv, xf_own, xn_send, xn_recv, xn_own,
    yn_send, yn_recv, z_send, z_recv, p_send, p_recv, p_own,
    yo_send, yo_recv, xo_send, xo_recv, xo_own,
):
    blocks = [early.at[k] if k < EARLY else late.at[k - EARLY] for k in range(NY)]
    chan, win = lax.axis_index("chan"), lax.axis_index("win")
    total = lax.axis_size("chan")
    xc = lax.rem(chan, NX)
    row = chan - xc
    has_down, has_up = chan >= NX, chan < total - NX
    down, up = jnp.maximum(chan - NX, 0), jnp.minimum(chan + NX, total - 1)

    def y_at(k):
        return lax.rem(win + DISTANCES[k] + NY, NY)

    def x_at(step):
        return lax.rem(xc + step, NX)

    others = [k for k in range(NY) if k != OWN]
    barrier = pltpu.get_barrier_semaphore()
    for k in others:
        pl.semaphore_signal(barrier, inc=1, device_id=(chan, y_at(k)), device_id_type=MESH)
    for step in range(1, NX):
        pl.semaphore_signal(barrier, inc=1, device_id=(row + x_at(step), win), device_id_type=MESH)
    for there, to in ((has_down, down), (has_up, up)):

        @pl.when(there)
        def _():
            pl.semaphore_signal(barrier, inc=1, device_id=(to, win), device_id_type=MESH)

    loads = []
    for source, buffer in (
        (fwd_ref, fwd_buf),
        *[(x_ref.at[:, pl.ds(b * BLOCK, BLOCK)], x_buf.at[b]) for b in range(B_DEV)],
        (inv_ref, inv_buf), (low_ref, low_s), (high_ref, high_s), (used_ref, used_s),
    ):
        loads.append(pltpu.make_async_copy(source, buffer, load_sem.at[len(loads)]))
        loads[-1].start()

    local = (pairs_ref[...] - (row * B_DEV - 16)) & (NBLK - 1)
    my_pairs = pl.ds(pl.multiple_of(xc * 8, 8), 8)
    pair_buf[my_pairs, :] = jnp.concatenate(
        [
            jnp.concatenate([local, jnp.zeros((2, 128 - PO), jnp.int32)], axis=1),
            jnp.zeros((6, 128), jnp.int32),
        ],
        axis=0,
    )

    def transform(b):
        spec = jnp.dot(
            x_buf[b].reshape(SEGS * BLOCK, NT), fwd_buf[...], preferred_element_type=jnp.float32
        )
        re, im = spec[:, :F], spec[:, F:]
        power = re * re + im * im
        level = jnp.mean(power, axis=-1, keepdims=True)
        factor = lax.rsqrt(power + 0.1 * level + 1e-06)
        re, im = re * factor, im * factor
        for seg in range(SEGS):
            re_s[pl.ds(seg, BLOCK, stride=SEGS), :] = re[seg * BLOCK : (seg + 1) * BLOCK]
            im_s[pl.ds(seg, BLOCK, stride=SEGS), :] = im[seg * BLOCK : (seg + 1) * BLOCK]
        both = jnp.concatenate(
            [re_s[...].reshape(NX * NY, 8, F), im_s[...].reshape(NX * NY, 8, F)], axis=1
        )
        slices[:, :, b] = both.astype(jnp.bfloat16).reshape(NY, NX, ROWS, F)

    far_copies = []

    def send_far(b):
        for k in range(FAR):
            copy = remote(
                slices.at[y_at(k), :, b], far_in.at[BACK[k], :, b],
                yf_send.at[k, b], yf_recv.at[BACK[k], b], chan, y_at(k),
            )
            copy.start()
            far_copies.append(copy)

    own_place = pl.ds((4 + xc) * B_DEV, B_DEV)

    def each_x(send):
        def body(step, carry):
            send(x_at(step))
            return carry

        lax.fori_loop(1, NX, body, 0)

    def send_near(half):
        lo = half * 2
        for k in range(EARLY, NY):
            n = k - EARLY
            there = pl.ds(xc * B_DEV + lo, 2)

            def send(to):
                remote(
                    slices.at[y_at(k), to, pl.ds(lo, 2)], near_in.at[n, there],
                    xn_send.at[n], xn_recv.at[n], row + to, win,
                ).start()

            each_x(send)
            pltpu.make_async_copy(
                slices.at[y_at(k), xc, pl.ds(lo, 2)], near_in.at[n, there], xn_own.at[n, half]
            ).start()

    def spread_x(k):
        held = far_in.at[k] if k < FAR else slices.at[win]

        def send(to):
            remote(
                held.at[to], blocks[k].at[own_place], xf_send.at[k], xf_recv.at[k], row + to, win
            ).start()

        each_x(send)
        pltpu.make_async_copy(held.at[xc], blocks[k].at[own_place], xf_own.at[k]).start()

    loads[0].wait()
    for b in range(B_DEV):
        loads[1 + b].wait()
        transform(b)
        if b == 0:
            pl.semaphore_wait(
                barrier, NY + NX - 2 + has_down.astype(jnp.int32) + has_up.astype(jnp.int32)
            )
        send_far(b)
        if b % 2:
            send_near(b // 2)
    spread_x(OWN)
    p_copies = []
    for step in range(1, NX):
        p_copies.append(
            remote(
                pair_buf.at[my_pairs], pair_buf.at[my_pairs], p_send.at[step], p_recv.at[step],
                row + x_at(step), win,
            )
        )
        p_copies[-1].start()

    def near_all(n):
        many = near_in.at[n, pl.ds(0, (NX - 1) * B_DEV)]
        return remote(many, many, xn_send.at[n], xn_recv.at[n], chan, win)

    row_place = pl.ds(16, NX * B_DEV)
    near_copies = []
    for k in range(EARLY, NY):
        n = k - EARLY
        near_all(n).wait_recv()
        for half in range(2):
            part = pl.ds(xc * B_DEV + half * 2, 2)
            pltpu.make_async_copy(
                slices.at[y_at(k), xc, pl.ds(half * 2, 2)], near_in.at[n, part], xn_own.at[n, half]
            ).wait()
        copy = remote(
            near_in.at[n], blocks[BACK[k]].at[row_place], yn_send.at[n],
            yn_recv.at[BACK[k] - EARLY], chan, y_at(k),
        )
        copy.start()
        near_copies.append(copy)

    def halo_copy(k, side):
        lo, there, to = ((16, 48, down), (32, 0, up))[side]
        return remote(
            blocks[k].at[pl.ds(lo, 16)], blocks[k].at[pl.ds(there, 16)],
            z_send.at[k, side], z_recv.at[k, side], to, win,
        )

    def halo(k):
        for side, there in enumerate((has_down, has_up)):

            @pl.when(there)
            def _():
                halo_copy(k, side).start()

    def halo_wait(k):
        for side, there in enumerate((has_up, has_down)):

            @pl.when(there)
            def _():
                halo_copy(k, side).wait_recv()

    def spread_all(k):
        many = blocks[k].at[pl.ds(0, (NX - 1) * B_DEV)]
        return remote(many, many, xf_send.at[k], xf_recv.at[k], chan, win)

    def row_there(k):
        spread_all(k).wait_recv()
        pltpu.make_async_copy(
            slices.at[win, xc], blocks[k].at[own_place], xf_own.at[k]
        ).wait()
        halo(k)

    row_there(OWN)
    for k in (1, 2, 0):
        for b in range(B_DEV):
            remote(
                slices.at[0, :, b], far_in.at[k, :, b], yf_send.at[k, b], yf_recv.at[k, b],
                chan, y_at(k),
            ).wait_recv()
        spread_x(k)

    for step in range(1, NX):
        frm = lax.rem(xc + NX - step, NX)
        theirs = pl.ds(pl.multiple_of(frm * 8, 8), 8)
        remote(
            pair_buf.at[theirs], pair_buf.at[theirs], p_send.at[step], p_recv.at[step],
            row + frm, win,
        ).wait_recv()
    to_smem = pltpu.make_async_copy(pair_buf, pair_idx, p_own)
    to_smem.start()
    to_smem.wait()

    for k in (1, 2, 0):
        row_there(k)
    for k in range(EARLY, NY):
        remote(
            near_in.at[0], blocks[k].at[row_place], yn_send.at[k - EARLY], yn_recv.at[k - EARLY],
            chan, y_at(k),
        ).wait_recv()
        halo(k)

    def accumulate(held, y, more):
        def owner(o, carry):
            for q in range(PO // NY):
                j = y * (PO // NY) + q
                a, b = pair_idx[o * 8, j], pair_idx[o * 8 + 1, j]
                first = held[:, a].astype(jnp.float32)
                second = held[:, b].astype(jnp.float32)
                a_re, a_im, b_re, b_im = first[:, :8], first[:, 8:], second[:, :8], second[:, 8:]
                real = jnp.sum(a_re * b_re + a_im * b_im, axis=0)
                imag = jnp.sum(a_re * b_im - a_im * b_re, axis=0)
                at = pl.ds(pl.multiple_of((y * PO + o * 4 + q) * 8, 8), 8)
                if more:
                    real, imag = re_acc[at, :] + real, im_acc[at, :] + imag
                re_acc[at, :] = real
                im_acc[at, :] = imag
            return carry

        lax.fori_loop(0, NX, owner, 0)

    for k in range(EARLY):
        halo_wait(k)

    def first_half(y, carry):
        accumulate(early, y, False)
        return carry

    lax.fori_loop(0, NY, first_half, 0)
    for k in range(EARLY, NY):
        halo_wait(k)

    loads[1 + B_DEV].wait()
    out_copies = {}
    for k in OUT_ORDER:
        y = y_at(k)
        accumulate(late, y, True)
        at = y * (PO * 8)
        cross = jnp.concatenate(
            [
                sum(s[pl.ds(at + seg, NX * 8, stride=SEGS), :] for seg in range(SEGS))
                for s in (re_acc, im_acc)
            ],
            axis=1,
        )
        stacks[y] = jnp.dot(
            cross, inv_buf[...], precision=lax.Precision.HIGHEST, preferred_element_type=jnp.float32
        ).reshape(NX, 8, LAGS)
        if k != OWN:
            out_copies[k] = remote(
                stacks.at[y], stacks_in.at[BACK[k]], yo_send.at[k], yo_recv.at[BACK[k]], chan, y
            )
            out_copies[k].start()

    def rows_all(k):
        many = rows_in.at[pl.ds(0, (NX - 1) * 8)]
        return remote(many, many, xo_send.at[k], xo_recv.at[k], chan, win)

    outs = []
    for k in (OWN, 6, 7, 4, 5, 1, 2, 0):
        if k != OWN:
            remote(
                stacks.at[0], stacks_in.at[k], yo_send.at[k], yo_recv.at[k], chan, y_at(k)
            ).wait_recv()
        held = stacks.at[win] if k == OWN else stacks_in.at[k]
        place = pl.ds(pl.multiple_of((y_at(k) * NX + xc) * 8, 8), 8)

        def send(to):
            remote(
                held.at[to], rows_in.at[place], xo_send.at[k], xo_recv.at[k], row + to, win
            ).start()

        each_x(send)
        outs.append(pltpu.make_async_copy(held.at[xc], rows_in.at[place], xo_own.at[k]))
        outs[-1].start()
    for own in outs:
        own.wait()
    for k in range(NY):
        rows_all(k).wait_recv()

    for load in loads[2 + B_DEV :]:
        load.wait()
    lag = lax.broadcasted_iota(jnp.int32, (NX * NY, LAGS), 1)
    for slot in range(PO // NY):
        here = win * (PO // NY) + slot
        high = jnp.where(here < used_s[0], high_s[here], 0)
        keep = (lag >= low_s[here]) & (lag < high)
        for c in range(2):
            rows = rows_in[pl.ds(slot * 2 + c, NX * NY, stride=8), :]
            out_ref[pl.ds(slot * BLOCK + c, NX * NY, stride=2), :] = jnp.where(keep, rows, 0.0)

    for copy in far_copies + near_copies + p_copies + list(out_copies.values()):
        copy.wait_send()
    for n in range(NY - EARLY):
        near_all(n).wait_send()
    for k in range(EARLY):
        spread_all(k).wait_send()
    for k in range(NY):
        rows_all(k).wait_send()
        for side, there in enumerate((has_down, has_up)):

            @pl.when(there)
            def _():
                halo_copy(k, side).wait_send()


def per_device(records, block_pairs, lag_low, lag_high, slot_count):
    dma = pltpu.SemaphoreType.DMA
    hbm = pl.BlockSpec(memory_space=pltpu.HBM)
    vmem = pl.BlockSpec(memory_space=pltpu.VMEM)
    share = PO // NY
    near = NY - EARLY
    bf16, f32, i32 = jnp.bfloat16, jnp.float32, jnp.int32
    out = pl.pallas_call(
        kernel,
        out_shape=jax.ShapeDtypeStruct((share * BLOCK, LAGS), f32),
        in_specs=[hbm] * 6 + [vmem],
        out_specs=vmem,
        scratch_shapes=[
            pltpu.VMEM((B_DEV, SEGS, BLOCK, NT), bf16),
            pltpu.VMEM((NT, 2 * F), bf16),
            pltpu.VMEM((2 * F, LAGS), f32),
            pltpu.SMEM((PO,), i32),
            pltpu.SMEM((PO,), i32),
            pltpu.SMEM((1,), i32),
            pltpu.VMEM((SEGS * BLOCK, F), f32),
            pltpu.VMEM((SEGS * BLOCK, F), f32),
            pltpu.VMEM((NY, NX, B_DEV, ROWS, F), bf16),
            pltpu.VMEM((FAR, NX, B_DEV, ROWS, F), bf16),
            pltpu.VMEM((near, NX * B_DEV, ROWS, F), bf16),
            pltpu.VMEM((EARLY, NBLK, ROWS, F), bf16),
            pltpu.VMEM((near, NBLK, ROWS, F), bf16),
            pltpu.VMEM((NX * PO * 8, F), f32),
            pltpu.VMEM((NX * PO * 8, F), f32),
            pltpu.VMEM((NX * 8, 128), i32),
            pltpu.SMEM((NX * 8, 128), i32),
            pltpu.VMEM((NY, NX, 8, LAGS), f32),
            pltpu.VMEM((NY, NX, 8, LAGS), f32),
            pltpu.VMEM((NY * NX * 8, LAGS), f32),
            dma((B_DEV + 5,)),
            dma((FAR, B_DEV)), dma((FAR, B_DEV)),
            dma((EARLY,)), dma((EARLY,)), dma((EARLY,)),
            dma((near,)), dma((near,)), dma((near, 2)),
            dma((near,)), dma((near,)),
            dma((NY, 2)), dma((NY, 2)),
            dma((NX,)), dma((NX,)), dma(()),
            dma((NY,)), dma((NY,)), dma((NY,)), dma((NY,)), dma((NY,)),
        ],
        compiler_params=pltpu.CompilerParams(
            collective_id=0, has_side_effects=True, vmem_limit_bytes=63 << 20
        ),
    )(
        records, jnp.asarray(forward_table()), jnp.asarray(inverse_table()), lag_low, lag_high,
        slot_count, block_pairs.T,
    )
    return out.reshape(share, BLOCK, LAGS)


def solution(mesh):
    in_specs = (P("win", "chan", None), P("chan", None), P("chan"), P("chan"), P("chan"))
    out_specs = P(("chan", "win"), None, None)
    return jax.shard_map(
        per_device, mesh=mesh, in_specs=in_specs, out_specs=out_specs, check_vma=False
    )
```

time: 302 us -> 62.1 us (0.21)
  waiting for transfers between devices: 146 us -> 0 us
  local copies, waits for them, and re-layouts: 86.2 us -> 1.67 us
  Pallas kernels: 0 us -> 59.3 us
  other arithmetic: 26.3 us -> 0 us
  starting transfers between devices: 23.5 us -> 0 us
  between operations: 14.2 us -> 0.66 us
  matrix products: 4.45 us -> 0 us
    reduce_scatter x1 -> x0, waiting for transfers between devices: 91 us -> none  [per_device(): summed = lax.psum_scatter(spectrum, 'win', scatter_dimension=0, tiled=True)]
    pallas_call x0 -> x1, Pallas kernels: none -> 59.3 us  [per_device(): pl.pallas_call(kernel, out_shape=jax.ShapeDtypeStruct((share * BLOCK, LAG...]
    ppermute x8 -> x0, waiting for transfers between devices: 54.8 us -> none  [shifted(): return lax.ppermute(block, axis, route)]
    gather x8 -> x0, local copies, waits for them, and re-layouts: 45.8 us -> none  [the longest x4 23.1 us: one_group(): first = jnp.take(blocks, pair_rows[:, 0], axis=1)]
    ppermute x8 -> x0, starting transfers between devices: 23.5 us -> none  [shifted(): return lax.ppermute(block, axis, route)]
    unnamed x17 -> x1, local copies, waits for them, and re-layouts: 19.8 us -> 1.67 us
    concatenate x2 -> x0, local copies, waits for them, and re-layouts: 16.7 us -> none  [per_device(): neighbourhood = jnp.concatenate(pieces, axis=1)]
    select_n x4 -> x0, other arithmetic: 10.6 us -> none  [one_group(): second = jnp.take(blocks, pair_rows[:, 1], axis=1)]
  transfers between devices with their start and end apart: 9 -> 0, of which waited for: 6 -> 0; matrix products, arithmetic and copies ran while one was open for 7% -> 0% of each run, Pallas kernels for 0% -> 0%
where the time goes in v2:
time: 62.1 us; the launch traced here: 61.6 us
  Pallas kernels  59.3 us (95%)
  local copies, waits for them, and re-layouts  1.67 us (3%)
  between operations  0.66 us (1%)
    pallas_call x1, Pallas kernels, per_device(): pl.pallas_call(kernel, out_shape=jax.ShapeDtypeStruct((share * BLOCK, LAG...  59.3 us
    unnamed x1, local copies, waits for them, and re-layouts  1.67 us

profile of v2, /device:TPU:1, one launch (start us, length us, event | category | flops | bytes accessed | tf_op | source)
XLA Modules:
  0.0 61.6 jit_solution(7455577121134469166)
XLA Ops:
  0.7 59.3 %shard_map.73 = f32[512,128]{1,0:T(8,128)} custom-call(bf16[4,512,512]{2,1,0:T(8,128)(2,1)} %x_ref.1, bf16[512,256]{1,0:T(8,128)(2,1)} %constant.4.clone.fwd_ref, f32[256,128]{1,0:T(8,128)} %constant.5.clone.inv_ref, s32[32]{0:T(128)} %low_ref.1, s32[32]{0:T(128)} %high_ref.1, s32[1]{0:T(128)S(6)} %copy.9.used_ref, s32[2,32]{1,0:T(2,128)} %bitcast.3), custom_call_target="tpu_custom_call" | custom-call | tf_op jit(solution)/shard_map/pallas_call | solution.py:391
  59.9 1.7 %copy.10 = f32[4,128,128]{2,1,0:T(8,128)} copy(f32[4,128,128]{2,1,0:T(8,128)} %bitcast.2) | data formatting | bytes 524288

commit v3 on v2

v3 whole, which is shorter than its diff:
```python
import math

import jax
import jax.numpy as jnp
import ml_dtypes
import numpy as np
from jax import lax
from jax.experimental import pallas as pl
from jax.experimental.pallas import tpu as pltpu
from jax.sharding import PartitionSpec as P

BLOCK = 128
NT = 512
F = 128
LAGS = 128
B_DEV = 4
PO = 32
NX = 8
NY = 8
SEGS = 4
ROWS = 16
NBLK = 64
MESH = pl.DeviceIdType.MESH
DISTANCES = (4, 3, -3, 0, 2, -2, 1, -1)
BACK = (0, 2, 1, 3, 5, 4, 7, 6)
OWN, EARLY = 3, 4
OUT_ORDER = (0, 1, 2, 4, 5, 6, 7, 3)


def forward_table():
    times = np.arange(NT, dtype=np.int64)[:, None]
    freqs = (NT // 32 + np.arange(F, dtype=np.int64))[None, :]
    phase = 2.0 * math.pi / NT * (times * freqs % NT)
    table = np.concatenate([np.cos(phase), -np.sin(phase)], axis=1)
    return table.astype(np.float32).astype(ml_dtypes.bfloat16)


def inverse_table():
    freqs = (NT // 32 + np.arange(F, dtype=np.int64))[:, None]
    shifts = (np.arange(LAGS, dtype=np.int64) - LAGS // 2)[None, :]
    phase = 2.0 * math.pi / NT * (freqs * shifts % NT)
    table = np.concatenate([np.cos(phase), -np.sin(phase)], axis=0)
    return (table / math.sqrt(F * SEGS * NY)).astype(np.float32)


def remote(src, dst, send, recv, chan, win):
    return pltpu.make_async_remote_copy(
        src_ref=src,
        dst_ref=dst,
        send_sem=send,
        recv_sem=recv,
        device_id=(chan, win),
        device_id_type=MESH,
    )


def kernel(
    x_ref, fwd_ref, inv_ref, pairs_ref,
    rows_in,
    x_buf, fwd_buf, inv_buf, re_s, im_s, slices, early, late, re_acc, im_acc,
    pair_buf, pair_idx, stacks,
    load_sem, in_send, in_recv, in_own, z_send, z_recv, p_send, p_recv, p_own,
    out_send, out_recv, out_own,
):
    blocks = [early.at[k] if k < EARLY else late.at[k - EARLY] for k in range(NY)]
    chan, win = lax.axis_index("chan"), lax.axis_index("win")
    total = lax.axis_size("chan")
    xc = lax.rem(chan, NX)
    row = chan - xc
    has_down, has_up = chan >= NX, chan < total - NX
    down, up = jnp.maximum(chan - NX, 0), jnp.minimum(chan + NX, total - 1)

    def y_at(k):
        return lax.rem(win + DISTANCES[k] + NY, NY)

    def x_at(step):
        return lax.rem(xc + step, NX)

    me = win * NX + xc
    barrier = pltpu.get_barrier_semaphore()

    def call(step, carry):
        other = lax.rem(me + step, NX * NY)
        pl.semaphore_signal(
            barrier, inc=1, device_id=(row + lax.rem(other, NX), other // NX), device_id_type=MESH
        )
        return carry

    lax.fori_loop(1, NX * NY, call, 0)
    for there, to in ((has_down, down), (has_up, up)):

        @pl.when(there)
        def _():
            pl.semaphore_signal(barrier, inc=1, device_id=(to, win), device_id_type=MESH)

    loads = []
    for source, buffer in (
        (fwd_ref, fwd_buf),
        *[(x_ref.at[:, pl.ds(b * BLOCK, BLOCK)], x_buf.at[b]) for b in range(B_DEV)],
        (inv_ref, inv_buf),
    ):
        loads.append(pltpu.make_async_copy(source, buffer, load_sem.at[len(loads)]))
        loads[-1].start()

    local = (pairs_ref[...] - (row * B_DEV - 16)) & (NBLK - 1)
    my_pairs = pl.ds(pl.multiple_of(xc * 8, 8), 8)
    pair_buf[my_pairs, :] = jnp.concatenate(
        [
            jnp.concatenate([local, jnp.zeros((2, 128 - PO), jnp.int32)], axis=1),
            jnp.zeros((6, 128), jnp.int32),
        ],
        axis=0,
    )

    def transform(b):
        spec = jnp.dot(
            x_buf[b].reshape(SEGS * BLOCK, NT), fwd_buf[...], preferred_element_type=jnp.float32
        )
        re, im = spec[:, :F], spec[:, F:]
        power = re * re + im * im
        level = jnp.mean(power, axis=-1, keepdims=True)
        factor = lax.rsqrt(power + 0.1 * level + 1e-06)
        re, im = re * factor, im * factor
        for seg in range(SEGS):
            re_s[pl.ds(seg, BLOCK, stride=SEGS), :] = re[seg * BLOCK : (seg + 1) * BLOCK]
            im_s[pl.ds(seg, BLOCK, stride=SEGS), :] = im[seg * BLOCK : (seg + 1) * BLOCK]
        both = jnp.concatenate(
            [re_s[...].reshape(NX * NY, 8, F), im_s[...].reshape(NX * NY, 8, F)], axis=1
        )
        slices[:, :, b] = both.astype(jnp.bfloat16).reshape(NY, NX, ROWS, F)

    own_place = pl.ds((4 + xc) * B_DEV, B_DEV)

    def each_x(first, send):
        def body(step, carry):
            send(x_at(step))
            return carry

        lax.fori_loop(first, NX, body, 0)

    def spread(k):
        def send(to):
            remote(
                slices.at[y_at(k), to], blocks[BACK[k]].at[own_place], in_send.at[k],
                in_recv.at[BACK[k]], row + to, y_at(k),
            ).start()

        each_x(1 if k == OWN else 0, send)

    def spread_all(k):
        many = blocks[k].at[pl.ds(0, (NX - 1 if k == OWN else NX) * B_DEV)]
        return remote(many, many, in_send.at[k], in_recv.at[k], chan, y_at(k))

    loads[0].wait()
    for b in range(B_DEV):
        loads[1 + b].wait()
        transform(b)
    pl.semaphore_wait(
        barrier, NX * NY - 1 + has_down.astype(jnp.int32) + has_up.astype(jnp.int32)
    )
    for k in (0, 1, 2, OWN):
        spread(k)
    own = pltpu.make_async_copy(slices.at[win, xc], blocks[OWN].at[own_place], in_own)
    own.start()
    p_copies = []
    for step in range(1, NX):
        p_copies.append(
            remote(
                pair_buf.at[my_pairs], pair_buf.at[my_pairs], p_send.at[step], p_recv.at[step],
                row + x_at(step), win,
            )
        )
        p_copies[-1].start()

    def halo_copy(k, side):
        lo, there, to = ((16, 48, down), (32, 0, up))[side]
        return remote(
            blocks[k].at[pl.ds(lo, 16)], blocks[k].at[pl.ds(there, 16)],
            z_send.at[k, side], z_recv.at[k, side], to, win,
        )

    def halo(k):
        for side, there in enumerate((has_down, has_up)):

            @pl.when(there)
            def _():
                halo_copy(k, side).start()

    def halo_wait(k):
        for side, there in enumerate((has_up, has_down)):

            @pl.when(there)
            def _():
                halo_copy(k, side).wait_recv()

    def row_there(k):
        spread_all(k).wait_recv()
        halo(k)

    own.wait()
    row_there(OWN)
    row_there(0)
    spread(4)
    spread(5)
    row_there(1)
    row_there(2)
    spread(6)
    spread(7)

    for step in range(1, NX):
        frm = lax.rem(xc + NX - step, NX)
        theirs = pl.ds(pl.multiple_of(frm * 8, 8), 8)
        remote(
            pair_buf.at[theirs], pair_buf.at[theirs], p_send.at[step], p_recv.at[step],
            row + frm, win,
        ).wait_recv()
    to_smem = pltpu.make_async_copy(pair_buf, pair_idx, p_own)
    to_smem.start()
    to_smem.wait()

    for k in range(EARLY, NY):
        row_there(k)

    def accumulate(held, y, more):
        def owner(o, carry):
            for q in range(PO // NY):
                j = y * (PO // NY) + q
                a, b = pair_idx[o * 8, j], pair_idx[o * 8 + 1, j]
                first = held[:, a].astype(jnp.float32)
                second = held[:, b].astype(jnp.float32)
                a_re, a_im, b_re, b_im = first[:, :8], first[:, 8:], second[:, :8], second[:, 8:]
                real = jnp.sum(a_re * b_re + a_im * b_im, axis=0)
                imag = jnp.sum(a_re * b_im - a_im * b_re, axis=0)
                at = pl.ds(pl.multiple_of((y * PO + o * 4 + q) * 8, 8), 8)
                if more:
                    real, imag = re_acc[at, :] + real, im_acc[at, :] + imag
                re_acc[at, :] = real
                im_acc[at, :] = imag
            return carry

        lax.fori_loop(0, NX, owner, 0)

    for k in range(EARLY):
        halo_wait(k)

    def first_half(y, carry):
        accumulate(early, y, False)
        return carry

    lax.fori_loop(0, NY, first_half, 0)
    for k in range(EARLY, NY):
        halo_wait(k)

    loads[1 + B_DEV].wait()
    my_rows = pl.ds(pl.multiple_of(me * 8, 8), 8)
    for k in OUT_ORDER:
        y = y_at(k)
        accumulate(late, y, True)
        at = y * (PO * 8)
        cross = jnp.concatenate(
            [
                sum(s[pl.ds(at + seg, NX * 8, stride=SEGS), :] for seg in range(SEGS))
                for s in (re_acc, im_acc)
            ],
            axis=1,
        )
        stacks[y] = jnp.dot(
            cross, inv_buf[...], precision=lax.Precision.HIGHEST, preferred_element_type=jnp.float32
        ).reshape(NX, 8, LAGS)

        def send(to):
            remote(
                stacks.at[y, to], rows_in.at[my_rows], out_send.at[k], out_recv, row + to, y
            ).start()

        each_x(1 if k == OWN else 0, send)
    out_copy = pltpu.make_async_copy(stacks.at[win, xc], rows_in.at[my_rows], out_own)
    out_copy.start()

    for copy in p_copies:
        copy.wait_send()
    for k in range(NY):
        spread_all(k).wait_send()
        many = rows_in.at[pl.ds(0, (NX - 1 if k == OWN else NX) * 8)]
        remote(many, many, out_send.at[k], out_recv, chan, win).wait_send()
        for side, there in enumerate((has_down, has_up)):

            @pl.when(there)
            def _():
                halo_copy(k, side).wait_send()

    out_copy.wait()
    many = rows_in.at[pl.ds(0, (NX * NY - 1) * 8)]
    remote(many, many, out_send.at[0], out_recv, chan, win).wait_recv()


def mask_kernel(low_ref, high_ref, used_ref, v_ref, out_ref):
    lag = lax.broadcasted_iota(jnp.int32, (NX * NY, LAGS), 1)
    start = lax.axis_index("win") * (PO // NY)
    for slot in range(PO // NY):
        here = start + slot
        high = jnp.where(here < used_ref[0], high_ref[here], 0)
        keep = (lag >= low_ref[here]) & (lag < high)
        for c in range(2):
            part = v_ref[pl.ds(slot * 2 + c, NX * NY, stride=8), :]
            out_ref[pl.ds(slot * BLOCK + c, NX * NY, stride=2), :] = jnp.where(keep, part, 0.0)


def masked(lag_low, lag_high, slot_count, rows):
    smem = pl.BlockSpec(memory_space=pltpu.SMEM)
    vmem = pl.BlockSpec(memory_space=pltpu.VMEM)
    share = PO // NY
    return pl.pallas_call(
        mask_kernel,
        out_shape=jax.ShapeDtypeStruct((share * BLOCK, LAGS), jnp.float32),
        in_specs=[smem, smem, smem, vmem],
        out_specs=vmem,
    )(lag_low, lag_high, slot_count, rows).reshape(
        share, BLOCK, LAGS
    )


def per_device(records, block_pairs, lag_low, lag_high, slot_count):
    dma = pltpu.SemaphoreType.DMA
    hbm = pl.BlockSpec(memory_space=pltpu.HBM)
    vmem = pl.BlockSpec(memory_space=pltpu.VMEM)
    near = NY - EARLY
    bf16, f32, i32 = jnp.bfloat16, jnp.float32, jnp.int32
    rows = pl.pallas_call(
        kernel,
        out_shape=jax.ShapeDtypeStruct((NY * NX * 8, LAGS), f32),
        in_specs=[hbm] * 3 + [vmem],
        out_specs=hbm,
        scratch_shapes=[
            pltpu.VMEM((B_DEV, SEGS, BLOCK, NT), bf16),
            pltpu.VMEM((NT, 2 * F), bf16),
            pltpu.VMEM((2 * F, LAGS), f32),
            pltpu.VMEM((SEGS * BLOCK, F), f32),
            pltpu.VMEM((SEGS * BLOCK, F), f32),
            pltpu.VMEM((NY, NX, B_DEV, ROWS, F), bf16),
            pltpu.VMEM((EARLY, NBLK, ROWS, F), bf16),
            pltpu.VMEM((near, NBLK, ROWS, F), bf16),
            pltpu.VMEM((NX * PO * 8, F), f32),
            pltpu.VMEM((NX * PO * 8, F), f32),
            pltpu.VMEM((NX * 8, 128), i32),
            pltpu.SMEM((NX * 8, 128), i32),
            pltpu.VMEM((NY, NX, 8, LAGS), f32),
            dma((B_DEV + 2,)),
            dma((NY,)), dma((NY,)), dma(()),
            dma((NY, 2)), dma((NY, 2)),
            dma((NX,)), dma((NX,)), dma(()),
            dma((NY,)), dma(()), dma(()),
        ],
        compiler_params=pltpu.CompilerParams(
            collective_id=0, has_side_effects=True, vmem_limit_bytes=63 << 20
        ),
    )(
        records, jnp.asarray(forward_table()), jnp.asarray(inverse_table()), block_pairs.T
    )
    return masked(lag_low, lag_high, slot_count, rows)


def solution(mesh):
    in_specs = (P("win", "chan", None), P("chan", None), P("chan"), P("chan"), P("chan"))
    out_specs = P(("chan", "win"), None, None)
    return jax.shard_map(
        per_device, mesh=mesh, in_specs=in_specs, out_specs=out_specs, check_vma=False
    )
```

time: 62.1 us -> 56.5 us (0.910)
  Pallas kernels: 59.3 us -> 55.3 us
  local copies, waits for them, and re-layouts: 1.67 us -> 0 us
    pallas_call x1 -> x2, Pallas kernels: 59.3 us -> 55.3 us  [the longest x1 53.6 us: per_device(): pl.pallas_call(kernel, out_shape=jax.ShapeDtypeStruct((NY * NX * 8, LAGS)...]
    unnamed x1 -> x0, local copies, waits for them, and re-layouts: 1.67 us -> none
where the time goes in v3:
time: 56.5 us; the launch traced here: 55.9 us
  Pallas kernels  55.3 us (98%)
  between operations  0.66 us (1%)
    pallas_call x1, Pallas kernels, per_device(): pl.pallas_call(kernel, out_shape=jax.ShapeDtypeStruct((NY * NX * 8, LAGS)...  53.6 us
    pallas_call x1, Pallas kernels, masked(): pl.pallas_call(mask_kernel, out_shape=jax.ShapeDtypeStruct((share * BLOCK...  1.73 us

profile of v3, /device:TPU:1, one launch (start us, length us, event | category | flops | bytes accessed | tf_op | source)
XLA Modules:
  0.0 55.9 jit_solution(12019784775530144740)
XLA Ops:
  0.7 53.6 %shard_map.73.v_ref = f32[512,128]{1,0:T(8,128)} custom-call(bf16[4,512,512]{2,1,0:T(8,128)(2,1)} %x_ref.1, bf16[512,256]{1,0:T(8,128)(2,1)} %constant.4.clone.fwd_ref, f32[256,128]{1,0:T(8,128)} %constant.5.clone.inv_ref, s32[2,32]{1,0:T(2,128)} %bitcast.2), custom_call_target="tpu_custom_call" | custom-call | tf_op jit(solution)/shard_map/pallas_call | solution.py:329
  54.2 1.7 %shard_map.74 = f32[512,128]{1,0:T(8,128)} custom-call(s32[32]{0:T(128)} %low_ref.1, s32[32]{0:T(128)} %high_ref.1, s32[1]{0:T(128)S(6)} %copy.8.used_ref, f32[512,128]{1,0:T(8,128)} %shard_map.73.v_ref), custom_call_target="tpu_custom_call" | custom-call | tf_op jit(solution)/shard_map/pallas_call | solution.py:313

commit v4 on v3

--- a/solution.py
+++ b/solution.py
@@ -21,10 +21,10 @@
 ROWS = 16
 NBLK = 64
 MESH = pl.DeviceIdType.MESH
-DISTANCES = (4, 3, -3, 0, 2, -2, 1, -1)
-BACK = (0, 2, 1, 3, 5, 4, 7, 6)
+DISTANCES = (1, -1, 2, 0, -2, 3, -3, 4)
+BACK = (1, 0, 4, 3, 2, 6, 5, 7)
 OWN, EARLY = 3, 4
-OUT_ORDER = (0, 1, 2, 4, 5, 6, 7, 3)
+OUT_ORDER = (7, 5, 6, 2, 4, 0, 1, 3)
 
 
 def forward_table():
@@ -158,7 +158,7 @@
     pl.semaphore_wait(
         barrier, NX * NY - 1 + has_down.astype(jnp.int32) + has_up.astype(jnp.int32)
     )
-    for k in (0, 1, 2, OWN):
+    for k in (0, 1, OWN, 2, 4, 5, 6, 7):
         spread(k)
     own = pltpu.make_async_copy(slices.at[win, xc], blocks[OWN].at[own_place], in_own)
     own.start()
@@ -198,14 +198,8 @@
         halo(k)
 
     own.wait()
-    row_there(OWN)
-    row_there(0)
-    spread(4)
-    spread(5)
-    row_there(1)
-    row_there(2)
-    spread(6)
-    spread(7)
+    for k in (0, 1, OWN, 2):
+        row_there(k)
 
     for step in range(1, NX):
         frm = lax.rem(xc + NX - step, NX)

time: 56.5 us -> 55.3 us (0.979)
  Pallas kernels: 55.3 us -> 54.1 us
    pallas_call x1, Pallas kernels: 53.6 us -> 52.3 us  [per_device(): pl.pallas_call(kernel, out_shape=jax.ShapeDtypeStruct((NY * NX * 8, LAGS)...]
where the time goes in v4:
time: 55.3 us; the launch traced here: 54.7 us
  Pallas kernels  54.1 us (98%)
  between operations  0.66 us (1%)
    pallas_call x1, Pallas kernels, per_device(): pl.pallas_call(kernel, out_shape=jax.ShapeDtypeStruct((NY * NX * 8, LAGS)...  52.3 us
    pallas_call x1, Pallas kernels, masked(): pl.pallas_call(mask_kernel, out_shape=jax.ShapeDtypeStruct((share * BLOCK...  1.73 us

profile of v4, /device:TPU:1, one launch (start us, length us, event | category | flops | bytes accessed | tf_op | source)
XLA Modules:
  0.0 54.7 jit_solution(1297814422162004162)
XLA Ops:
  0.7 52.3 %shard_map.73.v_ref = f32[512,128]{1,0:T(8,128)} custom-call(bf16[4,512,512]{2,1,0:T(8,128)(2,1)} %x_ref.1, bf16[512,256]{1,0:T(8,128)(2,1)} %constant.4.clone.fwd_ref, f32[256,128]{1,0:T(8,128)} %constant.5.clone.inv_ref, s32[2,32]{1,0:T(2,128)} %bitcast.2), custom_call_target="tpu_custom_call" | custom-call | tf_op jit(solution)/shard_map/pallas_call | solution.py:323
  53.0 1.7 %shard_map.74 = f32[512,128]{1,0:T(8,128)} custom-call(s32[32]{0:T(128)} %low_ref.1, s32[32]{0:T(128)} %high_ref.1, s32[1]{0:T(128)S(6)} %copy.8.used_ref, f32[512,128]{1,0:T(8,128)} %shard_map.73.v_ref), custom_call_target="tpu_custom_call" | custom-call | tf_op jit(solution)/shard_map/pallas_call | solution.py:307

commit v5 on v4

--- a/solution.py
+++ b/solution.py
@@ -158,7 +158,7 @@
     pl.semaphore_wait(
         barrier, NX * NY - 1 + has_down.astype(jnp.int32) + has_up.astype(jnp.int32)
     )
-    for k in (0, 1, OWN, 2, 4, 5, 6, 7):
+    for k in (OWN, 2, 4, 0, 1, 5, 6, 7):
         spread(k)
     own = pltpu.make_async_copy(slices.at[win, xc], blocks[OWN].at[own_place], in_own)
     own.start()
@@ -198,7 +198,7 @@
         halo(k)
 
     own.wait()
-    for k in (0, 1, OWN, 2):
+    for k in (OWN, 2, 4, 0, 1):
         row_there(k)
 
     for step in range(1, NX):
@@ -212,7 +212,7 @@
     to_smem.start()
     to_smem.wait()
 
-    for k in range(EARLY, NY):
+    for k in range(EARLY + 1, NY):
         row_there(k)
 
     def accumulate(held, y, more):

time: 55.3 us -> 54.9 us (level)
  no operation moved by 1% of the time
where the time goes in v5:
time: 54.9 us; the launch traced here: 54.3 us
  Pallas kernels  53.7 us (98%)
  between operations  0.66 us (1%)
    pallas_call x1, Pallas kernels, per_device(): pl.pallas_call(kernel, out_shape=jax.ShapeDtypeStruct((NY * NX * 8, LAGS)...  51.9 us
    pallas_call x1, Pallas kernels, masked(): pl.pallas_call(mask_kernel, out_shape=jax.ShapeDtypeStruct((share * BLOCK...  1.73 us

profile of v5, /device:TPU:1, one launch (start us, length us, event | category | flops | bytes accessed | tf_op | source)
XLA Modules:
  0.0 54.3 jit_solution(15115556787876028017)
XLA Ops:
  0.7 51.9 %shard_map.73.v_ref = f32[512,128]{1,0:T(8,128)} custom-call(bf16[4,512,512]{2,1,0:T(8,128)(2,1)} %x_ref.1, bf16[512,256]{1,0:T(8,128)(2,1)} %constant.4.clone.fwd_ref, f32[256,128]{1,0:T(8,128)} %constant.5.clone.inv_ref, s32[2,32]{1,0:T(2,128)} %bitcast.2), custom_call_target="tpu_custom_call" | custom-call | tf_op jit(solution)/shard_map/pallas_call | solution.py:323
  52.6 1.7 %shard_map.74 = f32[512,128]{1,0:T(8,128)} custom-call(s32[32]{0:T(128)} %low_ref.1, s32[32]{0:T(128)} %high_ref.1, s32[1]{0:T(128)S(6)} %copy.8.used_ref, f32[512,128]{1,0:T(8,128)} %shard_map.73.v_ref), custom_call_target="tpu_custom_call" | custom-call | tf_op jit(solution)/shard_map/pallas_call | solution.py:307
